TPU v7x, 32 devices: a whole 2x2x4 slice. The times are simulated.
32 devices in a mesh: groups: 2 (over y), rows: 4 (over z), mp: 2 (over x), pair: 2 (over core).
Axes of the slice: x: 2, y: 2, z: 4, core: 2. Of those that a mesh axis runs over, the one named last changes fastest.
Arguments:
- query_rows: bfloat16 [2048, 512], P(('groups', 'rows', 'pair'), 'mp'), parts along dimension 0, may hold values from -240 to 240
- key_rows: bfloat16 [65536, 512], P(('groups', 'rows', 'pair'), 'mp'), parts along dimension 0, may hold values from -24 to 24
- value_rows: bfloat16 [65536, 512], P(('groups', 'rows', 'pair'), 'mp'), parts along dimension 0, may hold values from -6 to 6
- cotangent: bfloat16 [2048, 512], P(('groups', 'rows', 'pair'), 'mp'), parts along dimension 0, may hold values from -1536 to 1536
- train_rows: int32 [16], P('groups'), parts along dimension 0, may hold values from 1 to 12288, as said below
- test_rows: int32 [16], P('groups'), parts along dimension 0, may hold values from 32 to 128
- block_table: int32 [128], P('groups'), parts along dimension 0, may hold values from 0 to 7, as said below
Outputs:
- query_grad: bfloat16 [2048, 512], P(('groups', 'rows', 'pair'), 'mp'), parts along dimension 0
- key_grad: bfloat16 [65536, 512], P(('groups', 'rows', 'pair'), 'mp'), parts along dimension 0
- value_grad: bfloat16 [65536, 512], P(('groups', 'rows', 'pair'), 'mp'), parts along dimension 0
There are 2 independent parts, one for each index of `groups`. A program takes and returns all parts, laid end to end along the dimension named above; each array names one. Nothing has to cross between parts.
Inputs may be any that keep to these rules, and one draw needn't show every extreme that they name: block_table names table t exactly ceil(train_rows[t] / 512) times; the largest table has 24 full blocks. `block_table`: every table is named at least once.
All inputs are finite; a program needn't handle non-finite values.
Results may differ from a plain program's by a relative error of at most 0.0075.
Values may be sent and summed in bfloat16 or wider, within the bound.
No kernel may reach another device: no remote copies, remote signals or barrier semaphores. Data moves between devices by JAX's collectives and lax.ppermute only.
A program may use at most 64 MiB of HBM per device.

v0:
```python
import math
import jax
import jax.numpy as jnp
from jax import lax
from jax.sharding import PartitionSpec as P

HD = 64
TEST = 128
BLK = 512
NEG = -1e30


def combined_all(value, axis, join):
    pieces = jax.tree.map(lambda part: lax.all_gather(part, axis), value)
    head = jax.tree.map(lambda part: part[0], pieces)
    tail = jax.tree.map(lambda part: part[1:], pieces)
    total, _ = lax.scan(lambda total, piece: (join(total, piece), None), head, tail)
    return total


def table_lookup(positions, entries):
    matches = positions[:, None] == jnp.arange(entries.shape[0], dtype=jnp.int32)[None, :]
    return jnp.sum(jnp.where(matches, entries[None, :], 0), axis=1)


def merge_two(former, latter):
    new_peak = jnp.maximum(former[0], latter[0])
    return (
        new_peak,
        former[1] * jnp.exp(former[0] - new_peak) + latter[1] * jnp.exp(latter[0] - new_peak),
    )


def contract_rows(left, right):
    return lax.dot_general(
        left, right, (((0,), (0,)), ((), ())), preferred_element_type=jnp.float32
    )


def contract_features(left, right):
    return lax.dot_general(
        left, right, (((1,), (1,)), ((), ())), preferred_element_type=jnp.float32
    )


def local(query_rows, key_rows, value_rows, cotangent, train_rows, test_rows, block_table):
    device = lax.axis_index(("rows", "pair"))
    local_rows = query_rows.shape[0]
    features = query_rows.shape[1]
    head_count = features // HD
    blocks = key_rows.shape[0] // BLK
    tables = train_rows.shape[0]
    query_count = tables * TEST
    stacked = head_count * TEST
    score_scale = 1.0 / math.sqrt(HD)
    row_ids = device * local_rows + jnp.arange(local_rows, dtype=jnp.int32)
    query_live = row_ids % TEST < table_lookup(row_ids // TEST, test_rows)
    live_grads = jnp.where(query_live[:, None], cotangent, jnp.zeros_like(cotangent))
    all_queries, all_grads = (
        lax.all_gather(query_rows, ("rows", "pair"), axis=0, tiled=True),
        lax.all_gather(live_grads, ("rows", "pair"), axis=0, tiled=True),
    )
    head_of_feature = jnp.arange(features, dtype=jnp.int32) // HD
    head_mask = head_of_feature[None, :] == jnp.arange(head_count, dtype=jnp.int32)[:, None]

    def expand(rows):
        shaped = rows.reshape(tables, 1, TEST, features)
        masked = jnp.where(head_mask[None, :, None, :], shaped, jnp.zeros_like(shaped))
        return masked.reshape(tables, stacked, features)

    def collapse(product):
        shaped = product.reshape(head_count, TEST, features)
        return jnp.sum(jnp.where(head_mask[:, None, :], shaped, 0.0), axis=0)

    spread_queries = expand(all_queries)
    spread_grads = expand(all_grads)
    block_ids = jnp.arange(block_table.shape[0], dtype=jnp.int32)
    my_blocks = device * blocks + jnp.arange(blocks, dtype=jnp.int32)
    block_owner = lax.dynamic_slice_in_dim(block_table, device * blocks, blocks)
    earlier = (block_table[None, :] == block_owner[:, None]) & (
        block_ids[None, :] < my_blocks[:, None]
    )
    ordinal = jnp.sum(jnp.where(earlier, 1, 0), axis=1).astype(jnp.int32)
    live_keys = table_lookup(block_owner, train_rows) - ordinal * BLK
    key_blocks = key_rows.reshape(blocks, BLK, features)
    value_blocks = value_rows.reshape(blocks, BLK, features)
    key_index = jnp.arange(BLK, dtype=jnp.int32)
    block_inputs = (block_owner, live_keys, key_blocks, value_blocks)

    def block_scores(which_table, live_count, key_block):
        query_block = spread_queries[which_table]
        raw_scores = contract_features(query_block, key_block) * score_scale
        return (query_block, jnp.where(key_index[None, :] < live_count, raw_scores, NEG))

    def stats_step(running, inputs):
        which_table, live_count, key_block, value_block = inputs
        _, scores = block_scores(which_table, live_count, key_block)
        block_peak = jnp.max(scores, axis=1)
        weights = jnp.exp(scores - block_peak[:, None])
        block_mass = jnp.sum(weights, axis=1)
        old_peak = running[0][which_table]
        old_mass = running[1][which_table]
        new_peak = jnp.maximum(old_peak, block_peak)
        old_weight = jnp.exp(old_peak - new_peak)
        new_weight = jnp.exp(block_peak - new_peak)
        updated = [
            running[0].at[which_table].set(new_peak),
            running[1].at[which_table].set(old_mass * old_weight + block_mass * new_weight),
        ]
        return (tuple(updated), None)

    initial = [
        jnp.full((tables, stacked), NEG, jnp.float32),
        jnp.zeros((tables, stacked), jnp.float32),
    ]
    result, _ = lax.scan(stats_step, tuple(initial), block_inputs)
    peaks, masses = result
    peaks, masses = combined_all((peaks, masses), ("rows", "pair"), merge_two)

    def inner_step(running, inputs):
        which_table, live_count, key_block, value_block = inputs
        _, scores = block_scores(which_table, live_count, key_block)
        dprobs = contract_features(spread_grads[which_table], value_block)
        block_peak = jnp.max(scores, axis=1)
        weights_low = jnp.exp(scores - block_peak[:, None]).astype(jnp.bfloat16).astype(jnp.float32)
        term = (
            jnp.sum(weights_low * dprobs, axis=1)
            * jnp.exp(block_peak - peaks[which_table])
            / masses[which_table]
        )
        return (running.at[which_table].add(term), None)

    inner_terms, _ = lax.scan(inner_step, jnp.zeros((tables, stacked), jnp.float32), block_inputs)
    inner = lax.psum(inner_terms, ("rows", "pair"))

    def grad_step(running, inputs):
        which_table, live_count, key_block, value_block = inputs
        query_block, scores = block_scores(which_table, live_count, key_block)
        grad_block = spread_grads[which_table]
        probs = jnp.exp(scores - peaks[which_table][:, None]) / masses[which_table][:, None]
        dprobs = contract_features(grad_block, value_block)
        probs_low = probs.astype(jnp.bfloat16)
        value_part = contract_rows(probs_low, grad_block)
        dscores = (probs * (dprobs - inner[which_table][:, None])).astype(jnp.bfloat16)
        key_part = contract_rows(dscores, query_block) * score_scale
        query_part = (
            collapse(jnp.dot(dscores, key_block, preferred_element_type=jnp.float32)) * score_scale
        )
        running = running.at[which_table].add(query_part)
        return (running, (key_part.astype(jnp.bfloat16), value_part.astype(jnp.bfloat16)))

    query_terms, (key_parts, value_parts) = lax.scan(
        grad_step, jnp.zeros((tables, TEST, features), jnp.float32), block_inputs
    )
    query_total = lax.psum_scatter(
        query_terms.reshape(query_count, features),
        ("rows", "pair"),
        scatter_dimension=0,
        tiled=True,
    )
    return (
        query_total.astype(jnp.bfloat16),
        key_parts.reshape(blocks * BLK, features),
        value_parts.reshape(blocks * BLK, features),
    )


def solution(mesh):
    in_specs = (
        P(("groups", "rows", "pair"), "mp"),
        P(("groups", "rows", "pair"), "mp"),
        P(("groups", "rows", "pair"), "mp"),
        P(("groups", "rows", "pair"), "mp"),
        P("groups"),
        P("groups"),
        P("groups"),
    )
    out_specs = (
        P(("groups", "rows", "pair"), "mp"),
        P(("groups", "rows", "pair"), "mp"),
        P(("groups", "rows", "pair"), "mp"),
    )
    return jax.shard_map(local, mesh=mesh, in_specs=in_specs, out_specs=out_specs, check_vma=False)
```

profile of v0, /device:TPU:0, one launch (start us, length us, event | category | flops | bytes accessed | tf_op | source)
XLA Modules:
  0.0 357.1 jit_solution(11898617688526695184)
XLA Ops:
  11.4 16.6 %all_gather.23 = bf16[1024,256]{1,0:T(8,128)(2,1)S(1)} all-gather(bf16[128,256]{1,0:T(8,128)(2,1)S(1)} %broadcast_select_fusion.3), channel_id=1, replica_groups=mesh['groups'=2,'rows'=4,'mp'=2,'pair'=2] {'rows','pair'}, dimensions={0}, use_global_device_ids=true | all-gather | bytes 589824 | tf_op jit(solution)/shard_map/all_gather | solution.py:61
  28.0 14.9 %all_gather.18 = bf16[1024,256]{1,0:T(8,128)(2,1)S(1)} all-gather(bf16[128,256]{1,0:T(8,128)(2,1)} %param.23), channel_id=1, replica_groups=mesh['groups'=2,'rows'=4,'mp'=2,'pair'=2] {'rows','pair'}, dimensions={0}, use_global_device_ids=true | all-gather | bytes 589824 | tf_op jit(solution)/shard_map/all_gather | solution.py:60
  42.9 1.7 bitcast_select_fusion
  44.6 55.1 %while.60 = (s32[]{:T(128)}, f32[8,512]{1,0:T(8,128)S(1)}, f32[8,512]{1,0:T(8,128)S(1)}, s32[8]{0:T(128)S(1)}, s32[8]{0:T(128)S(1)}, /*index=5*/bf16[8,512,256]{...) while((s32[]{:T(128)}, f32[8,512]{1,0:T(8,128)S(1)}, ...), condition=%wide.region_7.8_spmd.clone.clone, body=%wide.region_3.7_spmd.clone.sunk.clone | while | flops 135532048 | bytes 2649797 | solution.py:116
  99.8 14.2 %all-gather.1 = f32[64,512]{1,0:T(8,128)S(1)} all-gather(f32[8,512]{1,0:T(8,128)S(1)} %get-tuple-element.259), channel_id=3, replica_groups=mesh['groups'=2,'rows'=4,'mp'=2,'pair'=2] {'rows','pair'}, dimensions={0}, use_global_device_ids=true | all-gather | bytes 147456 | tf_op jit(solution)/shard_map/all_gather | solution.py:14
  114.0 14.0 %all-gather = f32[64,512]{1,0:T(8,128)S(1)} all-gather(f32[8,512]{1,0:T(8,128)S(1)} %get-tuple-element.258), channel_id=2, replica_groups=mesh['groups'=2,'rows'=4,'mp'=2,'pair'=2] {'rows','pair'}, dimensions={0}, use_global_device_ids=true | all-gather | bytes 147456 | tf_op jit(solution)/shard_map/all_gather | solution.py:14
  128.3 61.7 %while.61 = (s32[]{:T(128)}, f32[8,512]{1,0:T(8,128)S(1)}, s32[8]{0:T(128)S(1)}, s32[8]{0:T(128)S(1)}, bf16[8,512,256]{2,1,0:T(8,128)(2,1)}, /*index=5*/bf16[8,5...) while((s32[]{:T(128)}, f32[8,512]{1,0:T(8,128)S(1)}, ...), condition=%wide.region_14.15_spmd.clone.clone, body=%wide.region_10.14_spmd.clone.sunk.clone | while | flops 270534656 | bytes 3170525 | solution.py:133
  190.1 29.2 %psum.7 = f32[8,512]{1,0:T(8,128)S(1)} all-reduce(f32[8,512]{1,0:T(8,128)S(1)} %get-tuple-element.262), channel_id=1, replica_groups=mesh['groups'=2,'rows'=4,'mp'=2,'pair'=2] {'rows','pair'}, use_global_device_ids=true, to_apply=%region_15.16 | all-reduce | flops 4096 | bytes 32768 | tf_op jit(solution)/shard_map/psum | solution.py:134
  219.4 97.7 %while.62 = (s32[]{:T(128)}, f32[8,128,256]{2,1,0:T(8,128)S(1)}, bf16[8,512,256]{2,1,0:T(8,128)(2,1)}, bf16[8,512,256]{2,1,0:T(8,128)(2,1)}, s32[8]{0:T(128)S(1)...) while((s32[]{:T(128)}, f32[8,128,256]{2,1,0:T(8,128)S(1)}, ...), condition=%wide.region_19.20_spmd.clone.clone, body=%wide.region_16.19_spmd.clone.sunk.clone | while | flops 673908224 | bytes 7627025 | solution.py:152
  229.6 2.0 fusion.131
  236.0 1.5 fusion.127
  241.8 2.0 fusion.131
  248.3 1.5 fusion.127
  254.0 2.0 fusion.131
  260.5 1.5 fusion.127
  266.2 2.0 fusion.131
  272.7 1.5 fusion.127
  278.4 2.0 fusion.131
  284.9 1.5 fusion.127
  290.6 2.0 fusion.131
  302.9 2.0 fusion.131
  315.1 2.0 fusion.131
  318.1 30.6 %reduce-scatter.2.cloned.1.call-done = f32[128,256]{1,0:T(8,128)} async-done(((f32[1024,256]{1,0:T(8,128)}), f32[128,256]{1,0:T(8,128)}) %reduce-scatter.2.cloned.1.call-update) | async-done | bytes 131088 | tf_op jit(solution)/shard_map/reduce_scatter | solution.py:155
  348.7 1.5 convert_element_type.21
  (265 shorter events, 151.3 us)
Async XLA Ops:
  7.2 341.5 %reduce-scatter.2.cloned.1.call-start = ((), (), s32[]{:S(2)}) async-start(), calls=%async_computation.1 | async-start | bytes 1179648 | tf_op jit(solution)/shard_map/reduce_scatter | solution.py:155
  42.9 1.7 copy-start.1
  128.3 91.1 %copy-start.2 = (s32[3]{0:T(128)S(1)}, s32[3]{0:T(128)}, u32[]{:S(2)}) copy-start(s32[3]{0:T(128)} %constant.200.clone.2) | copy-start | bytes 40
  317.1 1.0 copy-start
Sparse Core Ops, SparseCore 0:
  318.2 30.4 reduce-scatter.1
where the time goes:
time: 360 us; the launch traced here: 357 us
  matrix products  89.4 us (25%)
  blocking collectives  89 us (25%)
  other arithmetic  55.6 us (15%)
  loops' own time  45.8 us (13%)
  local copies, waits for them, and re-layouts  32.5 us (9%)
  waiting for transfers between devices  30.6 us (8%)
  between operations  14.2 us (4%)
    dot_general x40, matrix products, contract_features(): lax.dot_general(left, right, (((1,), (1,)), ((), ())), preferred_element_...  54.7 us
    reduce_scatter x1, waiting for transfers between devices, local(): lax.psum_scatter(query_terms.reshape(query_count, features), ('rows', 'pa...  30.6 us
    psum x1, blocking collectives, local(): inner = lax.psum(inner_terms, ('rows', 'pair'))  29.2 us
    dynamic_slice x48, local copies, waits for them, and re-layouts, local(): result, _ = lax.scan(stats_step, tuple(initial), block_inputs)  29 us
    all_gather x2, blocking collectives, combined_all(): pieces = jax.tree.map(lambda part: lax.all_gather(part, axis), value)  28.2 us
    another operation x42, other arithmetic  27.8 us
    dot_general x16, matrix products, contract_rows(): lax.dot_general(left, right, (((0,), (0,)), ((), ())), preferred_element_...  24.6 us
    all_gather x1, blocking collectives, local(): lax.all_gather(live_grads, ('rows', 'pair'), axis=0, tiled=True)  16.6 us
  transfers between devices with their start and end apart: 1, of which 1 were waited for; matrix products, arithmetic and copies ran while one was open for 0% of the time, Pallas kernels for 0%

commit v1 on v0

--- a/solution.py
+++ b/solution.py
@@ -8,6 +8,11 @@
 TEST = 128
 BLK = 512
 NEG = -1e30
+
+
+def add_all(x, name):
+    pieces = lax.all_gather(x, name)
+    return jnp.sum(pieces, axis=0)
 
 
 def combined_all(value, axis, join):
@@ -131,7 +136,7 @@
         return (running.at[which_table].add(term), None)
 
     inner_terms, _ = lax.scan(inner_step, jnp.zeros((tables, stacked), jnp.float32), block_inputs)
-    inner = lax.psum(inner_terms, ("rows", "pair"))
+    inner = add_all(inner_terms, ("rows", "pair"))
 
     def grad_step(running, inputs):
         which_table, live_count, key_block, value_block = inputs

time: 360 us -> 348 us (0.967)
  blocking collectives: 89 us -> 73.7 us
    psum x1 -> x0, blocking collectives: 29.2 us -> none  [local(): inner = lax.psum(inner_terms, ('rows', 'pair'))]
    all_gather x0 -> x1, blocking collectives: none -> 14 us  [add_all(): pieces = lax.all_gather(x, name)]
where the time goes in v1:
time: 348 us; the launch traced here: 345 us
  matrix products  89.4 us (26%)
  blocking collectives  73.7 us (21%)
  other arithmetic  55.6 us (16%)
  loops' own time  45.8 us (13%)
  waiting for transfers between devices  33.7 us (10%)
  local copies, waits for them, and re-layouts  32.5 us (9%)
  between operations  14.2 us (4%)
    dot_general x40, matrix products, contract_features(): lax.dot_general(left, right, (((1,), (1,)), ((), ())), preferred_element_...  54.7 us
    reduce_scatter x1, waiting for transfers between devices, local(): lax.psum_scatter(query_terms.reshape(query_count, features), ('rows', 'pa...  33.7 us
    dynamic_slice x48, local copies, waits for them, and re-layouts, local(): result, _ = lax.scan(stats_step, tuple(initial), block_inputs)  29 us
    all_gather x2, blocking collectives, combined_all(): pieces = jax.tree.map(lambda part: lax.all_gather(part, axis), value)  28.2 us
    another operation x42, other arithmetic  27.8 us
    dot_general x16, matrix products, contract_rows(): lax.dot_general(left, right, (((0,), (0,)), ((), ())), preferred_element_...  24.6 us
    all_gather x1, blocking collectives, local(): lax.all_gather(live_grads, ('rows', 'pair'), axis=0, tiled=True)  16.6 us
    another operation x1, loops' own time, local(): result, _ = lax.scan(stats_step, tuple(initial), block_inputs)  15.3 us
  transfers between devices with their start and end apart: 1, of which 1 were waited for; matrix products, arithmetic and copies ran while one was open for 0% of the time, Pallas kernels for 0%

profile of v1, /device:TPU:0, one launch (start us, length us, event | category | flops | bytes accessed | tf_op | source)
XLA Modules:
  0.0 345.0 jit_solution(7053761417048738381)
XLA Ops:
  11.4 16.6 %all_gather.29 = bf16[1024,256]{1,0:T(8,128)(2,1)S(1)} all-gather(bf16[128,256]{1,0:T(8,128)(2,1)S(1)} %broadcast_select_fusion.3), channel_id=1, replica_groups=mesh['groups'=2,'rows'=4,'mp'=2,'pair'=2] {'rows','pair'}, dimensions={0}, use_global_device_ids=true | all-gather | bytes 589824 | tf_op jit(solution)/shard_map/all_gather | solution.py:66
  28.0 14.9 %all_gather.24 = bf16[1024,256]{1,0:T(8,128)(2,1)S(1)} all-gather(bf16[128,256]{1,0:T(8,128)(2,1)} %param.23), channel_id=1, replica_groups=mesh['groups'=2,'rows'=4,'mp'=2,'pair'=2] {'rows','pair'}, dimensions={0}, use_global_device_ids=true | all-gather | bytes 589824 | tf_op jit(solution)/shard_map/all_gather | solution.py:65
  42.9 1.7 bitcast_select_fusion
  44.6 55.1 %while.60 = (s32[]{:T(128)}, f32[8,512]{1,0:T(8,128)S(1)}, f32[8,512]{1,0:T(8,128)S(1)}, s32[8]{0:T(128)S(1)}, s32[8]{0:T(128)S(1)}, /*index=5*/bf16[8,512,256]{...) while((s32[]{:T(128)}, f32[8,512]{1,0:T(8,128)S(1)}, ...), condition=%wide.region_7.8_spmd.clone.clone, body=%wide.region_3.7_spmd.clone.sunk.clone | while | flops 135532048 | bytes 2649797 | solution.py:121
  99.8 14.2 %all-gather.1 = f32[64,512]{1,0:T(8,128)S(1)} all-gather(f32[8,512]{1,0:T(8,128)S(1)} %get-tuple-element.259), channel_id=3, replica_groups=mesh['groups'=2,'rows'=4,'mp'=2,'pair'=2] {'rows','pair'}, dimensions={0}, use_global_device_ids=true | all-gather | bytes 147456 | tf_op jit(solution)/shard_map/all_gather | solution.py:19
  114.0 14.0 %all-gather = f32[64,512]{1,0:T(8,128)S(1)} all-gather(f32[8,512]{1,0:T(8,128)S(1)} %get-tuple-element.258), channel_id=2, replica_groups=mesh['groups'=2,'rows'=4,'mp'=2,'pair'=2] {'rows','pair'}, dimensions={0}, use_global_device_ids=true | all-gather | bytes 147456 | tf_op jit(solution)/shard_map/all_gather | solution.py:19
  128.3 61.7 %while.61 = (s32[]{:T(128)}, f32[8,512]{1,0:T(8,128)S(1)}, s32[8]{0:T(128)S(1)}, s32[8]{0:T(128)S(1)}, bf16[8,512,256]{2,1,0:T(8,128)(2,1)}, /*index=5*/bf16[8,5...) while((s32[]{:T(128)}, f32[8,512]{1,0:T(8,128)S(1)}, ...), condition=%wide.region_14.15_spmd.clone.clone, body=%wide.region_10.14_spmd.clone.sunk.clone | while | flops 270534656 | bytes 3170525 | solution.py:138
  190.0 14.0 %all-gather.2 = f32[64,512]{1,0:T(8,128)S(1)} all-gather(f32[8,512]{1,0:T(8,128)S(1)} %get-tuple-element.262), channel_id=4, replica_groups=mesh['groups'=2,'rows'=4,'mp'=2,'pair'=2] {'rows','pair'}, dimensions={0}, use_global_device_ids=true | all-gather | bytes 147456 | tf_op jit(solution)/shard_map/all_gather | solution.py:14
  204.2 97.7 %while.62 = (s32[]{:T(128)}, f32[8,128,256]{2,1,0:T(8,128)S(1)}, bf16[8,512,256]{2,1,0:T(8,128)(2,1)}, bf16[8,512,256]{2,1,0:T(8,128)(2,1)}, s32[8]{0:T(128)S(1)...) while((s32[]{:T(128)}, f32[8,128,256]{2,1,0:T(8,128)S(1)}, ...), condition=%wide.region_19.20_spmd.clone.clone, body=%wide.region_16.19_spmd.clone.sunk.clone | while | flops 673908224 | bytes 7627025 | solution.py:157
  208.6 1.5 fusion.127
  214.4 2.0 fusion.131
  220.8 1.5 fusion.127
  226.6 2.0 fusion.131
  233.0 1.5 fusion.127
  238.8 2.0 fusion.131
  245.3 1.5 fusion.127
  251.0 2.0 fusion.131
  263.2 2.0 fusion.131
  269.7 1.5 fusion.127
  275.4 2.0 fusion.131
  287.7 2.0 fusion.131
  299.9 2.0 fusion.131
  302.9 33.7 %reduce-scatter.2.cloned.1.call-done = f32[128,256]{1,0:T(8,128)} async-done(((f32[1024,256]{1,0:T(8,128)}), f32[128,256]{1,0:T(8,128)}) %reduce-scatter.2.cloned.1.call-update) | async-done | bytes 131088 | tf_op jit(solution)/shard_map/reduce_scatter | solution.py:160
  336.6 1.5 convert_element_type.21
  (266 shorter events, 151.3 us)
Async XLA Ops:
  7.2 329.4 %reduce-scatter.2.cloned.1.call-start = ((), (), s32[]{:S(2)}) async-start(), calls=%async_computation.1 | async-start | bytes 1179648 | tf_op jit(solution)/shard_map/reduce_scatter | solution.py:160
  42.9 1.7 copy-start.1
  128.3 75.8 %copy-start.2 = (s32[3]{0:T(128)S(1)}, s32[3]{0:T(128)}, u32[]{:S(2)}) copy-start(s32[3]{0:T(128)} %constant.201.clone.2) | copy-start | bytes 40
  301.9 1.0 copy-start
Sparse Core Ops, SparseCore 0:
  303.0 33.5 reduce-scatter.1
